TPU v7x, 32 devices: a whole 2x2x4 slice. The times are simulated.
32 devices in a mesh: freq: 4 (over x, core), rcv: 8 (over z, y).
Axes of the slice: x: 2, y: 2, z: 4, core: 2. Of those that a mesh axis runs over, the one named last changes fastest.
Arguments:
- reflection: bfloat16 [8, 2, 2560, 2560], P('freq', None, 'rcv'), may hold values from -5 to 5, as said below
- starts: int32 [2560, 192], P('rcv'), may hold values from 8 to 56
- focusing: float32 [8, 2560, 2, 192], P('freq', 'rcv'), may hold values from -6 to 6
- residual: float32 [8, 2560, 2, 192], P('freq', 'rcv'), may hold values from -6 to 6
- direction: float32 [8, 2560, 2, 192], P('freq', 'rcv'), may hold values from -6 to 6
- gradient: float32 [8, 2560, 2, 192], P('freq', 'rcv'), may hold values from -30 to 30
Outputs:
- new_focusing: float32 [8, 2560, 2, 192], P('freq', 'rcv')
- new_residual: float32 [8, 2560, 2, 192], P('freq', 'rcv')
- new_direction: float32 [8, 2560, 2, 192], P('freq', 'rcv')
- green_field: float32 [8, 2560, 2, 192], P('freq', 'rcv')
- focal_correlation: float32 [8, 2, 192], P('freq')
Inputs may be any that keep to these rules, and one draw needn't show every extreme that they name: Each frequency's matrix is symmetric in source and receiver: reflection[f, c, s, r] = reflection[f, c, r, s].
All inputs are finite; a program needn't handle non-finite values.
Results may differ from a plain program's by a relative error of at most 0.0003.
The roundings to bfloat16 on the way count: a program that leaves them out, or rounds other values in their place, can miss the bound.
Values may be sent and summed in bfloat16 or wider, within the bound.
No kernel may reach another device: no remote copies, remote signals or barrier semaphores. Data moves between devices by JAX's collectives and lax.ppermute only.
A program may use at most 64 MiB of HBM per device.

v0:
```python
import math
import jax
import jax.numpy as jnp
from jax import lax
from jax.sharding import PartitionSpec as P

N = 2560
F = 8
TS = 64
band_start = 5
tiny = 1e-06
highest = lax.Precision.HIGHEST


def tables(count):
    times = jnp.arange(TS, dtype=jnp.float32)[:, None]
    bins = (jnp.arange(count, dtype=jnp.int32) + band_start).astype(jnp.float32)[None, :]
    phase = 2.0 * jnp.pi * times * bins / TS
    return (jnp.cos(phase), jnp.sin(phase))


def contract_time(table, values):
    return jnp.einsum("tf,frk->trk", table, values, precision=highest)


def contract_back(table, values):
    return jnp.einsum("tf,trk->frk", table, values, precision=highest)


def time_gate(field, forward_cos, forward_sin, back_cos, back_sin, limits, complement):
    real_part = field[:, :, 0]
    imag_part = field[:, :, 1]
    time_real = contract_time(forward_cos, real_part) - contract_time(forward_sin, imag_part)
    time_imag = contract_time(forward_sin, real_part) + contract_time(forward_cos, imag_part)
    clock = jnp.arange(TS, dtype=jnp.int32)[:, None, None]
    window = (clock < limits[None]).astype(jnp.float32)
    if complement:
        window = 1.0 - window
    kept_real = window * time_real
    kept_imag = window * time_imag
    out_real = (contract_back(back_cos, kept_real) + contract_back(back_sin, kept_imag)) / TS
    out_imag = (contract_back(back_cos, kept_imag) - contract_back(back_sin, kept_real)) / TS
    return jnp.stack([out_real, out_imag], axis=2)


def combine(total, conjugate):
    if conjugate:
        out_real = total[:, 0, :, 0] + total[:, 1, :, 1]
        out_imag = total[:, 0, :, 1] - total[:, 1, :, 0]
    else:
        out_real = total[:, 0, :, 0] - total[:, 1, :, 1]
        out_imag = total[:, 0, :, 1] + total[:, 1, :, 0]
    return jnp.stack([out_real, out_imag], axis=2)


def per_device(reflection, starts, focusing, residual, direction, gradient):
    local_rows = reflection.shape[2]
    groups = lax.axis_size("freq")
    position = lax.axis_index("freq")
    cos_table, sin_table = tables(F)

    def gate(field, complement):
        spread = lax.all_to_all(field, "freq", split_axis=1, concat_axis=0, tiled=True)
        share = local_rows // groups
        limits = lax.dynamic_slice_in_dim(starts, position * share, share, 0)
        gated_part = time_gate(
            spread, cos_table, sin_table, cos_table, sin_table, limits, complement
        )
        return lax.all_to_all(gated_part, "freq", split_axis=0, concat_axis=1, tiled=True)

    def accumulate(piece):
        return jnp.einsum("fpnm,fmqk->fpnqk", reflection, piece, preferred_element_type=jnp.float32)

    direction_low = direction.astype(jnp.bfloat16)
    focusing_low = focusing.astype(jnp.bfloat16)
    aimed_total = accumulate(lax.all_gather(direction_low, "rcv", axis=1, tiled=True))
    direction_image = combine(aimed_total, False)
    gamma = lax.psum(jnp.sum(gradient * gradient), ("freq", "rcv"))
    image = gate(direction_image, False)
    curvature = lax.psum(jnp.sum(image * image), ("freq", "rcv"))
    alpha = gamma / (curvature + tiny)
    new_focusing = focusing + alpha * direction
    new_residual = residual - alpha * image
    gated = gate(new_residual, False).astype(jnp.bfloat16)
    total = accumulate(lax.all_gather(gated, "rcv", axis=1, tiled=True))
    new_gradient = combine(total, True)
    new_gamma = lax.psum(jnp.sum(new_gradient * new_gradient), ("freq", "rcv"))
    new_direction = new_gradient + new_gamma / (gamma + tiny) * direction
    focus_total = accumulate(lax.all_gather(focusing_low, "rcv", axis=1, tiled=True))
    focusing_image = combine(focus_total, False)
    green_field = gate(focusing_image + alpha * direction_image, True)
    corr_real = jnp.sum(
        green_field[:, :, 0] * new_focusing[:, :, 0] + green_field[:, :, 1] * new_focusing[:, :, 1],
        axis=1,
    )
    corr_imag = jnp.sum(
        green_field[:, :, 1] * new_focusing[:, :, 0] - green_field[:, :, 0] * new_focusing[:, :, 1],
        axis=1,
    )
    partial_corr = jnp.stack([corr_real, corr_imag], axis=1)
    focal_correlation = lax.psum(partial_corr, "rcv") / math.sqrt(N)
    return (new_focusing, new_residual, new_direction, green_field, focal_correlation)


def solution(mesh):
    return jax.shard_map(
        per_device,
        mesh=mesh,
        in_specs=(
            P("freq", None, "rcv", None),
            P("rcv", None),
            P("freq", "rcv", None, None),
            P("freq", "rcv", None, None),
            P("freq", "rcv", None, None),
            P("freq", "rcv", None, None),
        ),
        out_specs=(
            P("freq", "rcv", None, None),
            P("freq", "rcv", None, None),
            P("freq", "rcv", None, None),
            P("freq", "rcv", None, None),
            P("freq", None, None),
        ),
        check_vma=False,
    )
```

profile of v0, /device:TPU:0, one launch (start us, length us, event | category | flops | bytes accessed | tf_op | source)
XLA Modules:
  0.0 475.7 jit_solution(8466674727431938095)
XLA Ops:
  10.4 89.0 %all-gather.4.cloned.1.call-done = bf16[2,2560,2,192]{3,2,0,1:T(2,128)(2,1)} async-done(((bf16[2,320,2,192]{3,2,0,1:T(2,128)(2,1)}), bf16[2,2560,2,192]{3,2,0,1:T(2,128)(2,1)}) %all-gather.4.cloned.1.call-update) | async-done | bytes 3932176 | tf_op jit(solution)/shard_map/all_gather | solution.py:76
  99.4 8.1 %fusion.2 = f32[2,2,320,2,192]{2,4,3,1,0:T(8,128)S(1)} fusion(bf16[2,2,320,2560]{3,2,1,0:T(8,128)(2,1)} %param.6, bf16[2,2560,2,192,1]{3,2,0,1,4:T(2,128)(2,1)} %bitcast.192), kind=kOutput, calls=%fused_computation.2 | convolution fusion | flops 2516582400 | bytes 12451840 | tf_op jit(solution)/shard_map/fpnm,fmqk->fpnqk/dot_general | solution.py:72
  109.7 3.5 all-to-all-start
  117.2 13.3 %all-to-all-done = f32[2,320,2,192]{3,0,2,1:T(2,128)S(1)} async-done(((f32[2,320,2,192]{3,0,2,1:T(2,128)}), f32[2,320,2,192]{3,0,2,1:T(2,128)S(1)}, u32[]{:S(2)}, u32[]{:S(2)}) %all-to-all-start) | async-done | bytes 983072 | tf_op jit(solution)/shard_map/all_to_all | solution.py:63
  132.6 4.4 fusion.27
  137.1 4.4 fusion.26
  141.5 5.0 %subtract_select_fusion.1 = f32[64,80,192]{2,0,1:T(8,128)S(1)} fusion(f32[64,80,192]{2,0,1:T(8,128)S(1)} %fusion.27, s32[80,192]{1,0:T(8,128)S(1)} %copy.102, f32[8,80,2,192]{3,0,1,2:T(8,128)S(1)} %all_to_all.69, f32[8]{0:T(128)S(1)} %add_convert_fusion, f32[64]{0:T(128)S(1)} %iota_multiply_fusion), kind=kOutput, calls=%fused_computation.15 | convolution fusion | flops 97321984 | bytes 9913344 | tf_op jit(solution)/shard_map/tf,frk->trk/dot_general | solution.py:23
  149.2 4.9 %add_select_fusion.1 = f32[64,80,192]{2,0,1:T(8,128)S(1)} fusion(f32[64,80,192]{2,0,1:T(8,128)S(1)} %fusion.26, s32[80,192]{1,0:T(8,128)S(1)} %copy.102, f32[8,80,2,192]{3,0,1,2:T(8,128)S(1)} %all_to_all.69, f32[8]{0:T(128)S(1)} %add_convert_fusion, f32[64]{0:T(128)S(1)} %iota_multiply_fusion), kind=kOutput, calls=%fused_computation.14 | convolution fusion | flops 97321984 | bytes 9913344 | tf_op jit(solution)/shard_map/tf,frk->trk/dot_general | solution.py:23
  154.1 2.9 fusion.25
  163.8 3.5 all-to-all-start.1
  168.3 16.2 %all-to-all-done.1 = f32[8,80,2,192]{3,1,2,0:T(8,128)S(1)} async-done(((f32[8,80,2,192]{3,1,2,0:T(8,128)}), f32[8,80,2,192]{3,1,2,0:T(8,128)S(1)}, u32[]{:S(2)}, u32[]{:S(2)}) %all-to-all-start.1) | async-done | bytes 983072 | tf_op jit(solution)/shard_map/all_to_all | solution.py:69
  187.2 38.8 %all-reduce = (f32[]{:T(128)}, f32[]{:T(128)}) all-reduce(f32[]{:T(128)} %multiply_reduce_fusion.2, f32[]{:T(128)} %multiply_reduce_fusion), channel_id=1, replica_groups=mesh['freq'=4,'rcv'=8] {'freq','rcv'}, use_global_device_ids=true, to_apply=%region_1.0 | all-reduce | flops 2 | bytes 16 | tf_op jit(solution)/shard_map/psum | solution.py:78
  228.7 20.6 %all_to_all.90 = f32[2,320,2,192]{3,2,0,1:T(2,128)S(1)} all-to-all(f32[2,320,2,192]{3,2,0,1:T(2,128)S(1)} %copy.115), channel_id=1, replica_groups=mesh['freq'=4,'rcv'=8] {'freq'}, dimensions={1} | all-to-all | bytes 1966080 | tf_op jit(solution)/shard_map/all_to_all | solution.py:63
  254.2 4.4 fusion.29
  258.7 4.4 fusion.28
  263.1 5.0 %subtract_select_fusion = f32[64,80,192]{2,0,1:T(8,128)S(1)} fusion(f32[64,80,192]{2,0,1:T(8,128)S(1)} %fusion.29, s32[80,192]{1,0:T(8,128)S(1)} %copy.102, f32[8,80,2,192]{3,0,1,2:T(8,128)S(1)} %all_to_all.74, f32[8]{0:T(128)S(1)} %add_convert_fusion, f32[64]{0:T(128)S(1)} %iota_multiply_fusion), kind=kOutput, calls=%fused_computation.13 | convolution fusion | flops 97321984 | bytes 9913344 | tf_op jit(solution)/shard_map/tf,frk->trk/dot_general | solution.py:23
  270.8 4.9 %add_select_fusion = f32[64,80,192]{2,0,1:T(8,128)S(1)} fusion(f32[64,80,192]{2,0,1:T(8,128)S(1)} %fusion.28, s32[80,192]{1,0:T(8,128)S(1)} %copy.102, f32[8,80,2,192]{3,0,1,2:T(8,128)S(1)} %all_to_all.74, f32[8]{0:T(128)S(1)} %add_convert_fusion, f32[64]{0:T(128)S(1)} %iota_multiply_fusion), kind=kOutput, calls=%fused_computation.12 | convolution fusion | flops 97321984 | bytes 9913344 | tf_op jit(solution)/shard_map/tf,frk->trk/dot_general | solution.py:23
  278.3 2.8 fusion.58
  284.0 12.6 %all_to_all.91 = bf16[8,80,2,192]{3,1,2,0:T(8,128)(2,1)S(1)} all-to-all(bf16[8,80,2,192]{3,1,2,0:T(8,128)(2,1)S(1)} %copy.118), channel_id=1, replica_groups=mesh['freq'=4,'rcv'=8] {'freq'}, dimensions={0} | all-to-all | bytes 983040 | tf_op jit(solution)/shard_map/all_to_all | solution.py:69
  298.3 8.2 %fusion.4 = f32[2,2,320,2,192]{2,4,0,3,1:T(8,128)S(1)} fusion(bf16[2,2560,2,192,1]{3,2,0,1,4:T(2,128)(2,1)} %bitcast.190, bf16[2,2,320,2560]{3,2,1,0:T(8,128)(2,1)} %param.6), kind=kOutput, calls=%fused_computation.4 | convolution fusion | flops 2516582400 | bytes 12451840 | tf_op jit(solution)/shard_map/fpnm,fmqk->fpnqk/dot_general | solution.py:72
  310.4 19.7 %all_to_all.92 = f32[2,320,2,192]{3,0,2,1:T(2,128)S(1)} all-to-all(f32[2,320,2,192]{3,0,2,1:T(2,128)S(1)} %copy.131), channel_id=1, replica_groups=mesh['freq'=4,'rcv'=8] {'freq'}, dimensions={1} | all-to-all | bytes 1966080 | tf_op jit(solution)/shard_map/all_to_all | solution.py:63
  335.0 4.4 fusion.31
  339.4 4.4 fusion.30
  343.8 5.4 %subtract_multiply_fusion = f32[64,80,192]{2,0,1:T(8,128)S(1)} fusion(f32[64,80,192]{2,0,1:T(8,128)S(1)} %fusion.31, s32[80,192]{1,0:T(8,128)S(1)} %copy.102, f32[8,80,2,192]{3,0,1,2:T(8,128)S(1)} %all_to_all.79, f32[8]{0:T(128)S(1)} %add_convert_fusion, f32[64]{0:T(128)S(1)} %iota_multiply_fusion), kind=kOutput, calls=%fused_computation.10 | convolution fusion | flops 99288064 | bytes 9913344 | tf_op jit(solution)/shard_map/tf,frk->trk/dot_general | solution.py:23
  351.9 5.2 %add_multiply_fusion = f32[64,80,192]{2,0,1:T(8,128)S(1)} fusion(f32[64,80,192]{2,0,1:T(8,128)S(1)} %fusion.30, s32[80,192]{1,0:T(8,128)S(1)} %copy.102, f32[8,80,2,192]{3,0,1,2:T(8,128)S(1)} %all_to_all.79, f32[8]{0:T(128)S(1)} %add_convert_fusion, f32[64]{0:T(128)S(1)} %iota_multiply_fusion), kind=kOutput, calls=%fused_computation.9 | convolution fusion | flops 99288064 | bytes 9913344 | tf_op jit(solution)/shard_map/tf,frk->trk/dot_general | solution.py:23
  359.8 2.8 fusion.52
  362.6 2.7 fusion.15
  366.9 3.5 all-to-all-start.5
  372.5 15.1 %all-to-all-done.5 = f32[8,80,2,192]{3,1,2,0:T(8,128)S(1)} async-done(((f32[8,80,2,192]{3,1,2,0:T(8,128)}), f32[8,80,2,192]{3,1,2,0:T(8,128)S(1)}, u32[]{:S(2)}, u32[]{:S(2)}) %all-to-all-start.5) | async-done | bytes 983072 | tf_op jit(solution)/shard_map/all_to_all | solution.py:69
  390.4 10.1 %fusion.9 = f32[2,2,320,2,192]{2,4,1,3,0:T(8,128)S(1)} fusion(bf16[2,2,320,2560]{3,2,1,0:T(8,128)(2,1)} %param.6, bf16[2,2560,2,192,1]{3,2,0,1,4:T(2,128)(2,1)} %bitcast.191), kind=kOutput, calls=%fused_computation.17 | convolution fusion | flops 2516582400 | bytes 12451840 | tf_op jit(solution)/shard_map/fpnm,fmqk->fpnqk/dot_general | solution.py:72
  402.7 39.1 %psum.30 = f32[]{:T(128)} all-reduce(f32[]{:T(128)} %multiply_reduce_fusion.1), channel_id=1, replica_groups=mesh['freq'=4,'rcv'=8] {'freq','rcv'}, use_global_device_ids=true, to_apply=%region_5.0 | all-reduce | flops 1 | bytes 8 | tf_op jit(solution)/shard_map/psum | solution.py:87
  446.5 20.7 %psum.31 = f32[2,2,192]{2,0,1:T(2,128)S(1)} all-reduce(f32[2,2,192]{2,0,1:T(2,128)S(1)} %pad_maximum_fusion.5), channel_id=1, replica_groups=mesh['freq'=4,'rcv'=8] {'rcv'}, use_global_device_ids=true, to_apply=%region_8.0 | all-reduce | flops 768 | bytes 6144 | tf_op jit(solution)/shard_map/psum | solution.py:101
  (89 shorter events, 68.2 us)
Async XLA Ops:
  7.2 109.8 %copy-start = (s32[320,192]{0,1:T(8,128)S(1)}, s32[320,192]{0,1:T(8,128)}, u32[]{:S(2)}) copy-start(s32[320,192]{0,1:T(8,128)} %param.7) | copy-start | bytes 737284
  7.2 92.2 %all-gather.4.cloned.1.call-start = ((), (), s32[]{:S(2)}) async-start(), calls=%async_computation.6 | async-start | bytes 5898240 | tf_op jit(solution)/shard_map/all_gather | solution.py:76
  107.6 9.2 %copy-start.2 = (f32[2,320,1,192]{1,3,0,2:T(8,128)}, f32[2,320,1,192]{1,3,0,2:T(8,128)S(1)}, u32[]{:S(2)}) copy-start(f32[2,320,1,192]{1,3,0,2:T(8,128)S(1)} %fusion.39) | copy-start | bytes 1474564
  109.7 20.8 %all-to-all-start = ((f32[2,320,2,192]{3,0,2,1:T(2,128)}), f32[2,320,2,192]{3,0,2,1:T(2,128)S(1)}, u32[]{:S(2)}, u32[]{:S(2)}) async-start(f32[2,320,2,192]{3,0,2,1:T(2,128)} %copy.107), calls=%async_computation | async-start | bytes 2621440 | tf_op jit(solution)/shard_map/all_to_all | solution.py:63
  113.3 185.0 %all-gather.8.cloned.1.call-start = ((), (), s32[]{:S(2)}) async-start(), calls=%async_computation.8 | async-start | bytes 5898240 | tf_op jit(solution)/shard_map/all_gather | solution.py:89
  162.2 5.2 %copy-start.8 = (f32[2,320,2,192]{1,3,2,0:T(8,128)S(1)}, f32[2,320,2,192]{1,3,2,0:T(8,128)}, u32[]{:S(2)}) copy-start(f32[2,320,2,192]{1,3,2,0:T(8,128)} %param.11) | copy-start | bytes 2949124
  163.8 20.8 %all-to-all-start.1 = ((f32[8,80,2,192]{3,1,2,0:T(8,128)}), f32[8,80,2,192]{3,1,2,0:T(8,128)S(1)}, u32[]{:S(2)}, u32[]{:S(2)}) async-start(f32[8,80,2,192]{3,1,2,0:T(8,128)} %copy.110), calls=%async_computation.1 | async-start | bytes 2621440 | tf_op jit(solution)/shard_map/all_to_all | solution.py:69
  167.4 223.1 %all-gather.6.cloned.1.call-start = ((), (), s32[]{:S(2)}) async-start(), calls=%async_computation.7 | async-start | bytes 5898240 | tf_op jit(solution)/shard_map/all_gather | solution.py:85
  298.3 8.3 %copy-start.3 = (f32[2,320,1,192]{1,3,0,2:T(8,128)S(1)}, f32[2,320,1,192]{1,3,0,2:T(8,128)}, u32[]{:S(2)}) copy-start(f32[2,320,1,192]{1,3,0,2:T(8,128)} %copy-done.2) | copy-start | bytes 1474564
  366.9 20.8 %all-to-all-start.5 = ((f32[8,80,2,192]{3,1,2,0:T(8,128)}), f32[8,80,2,192]{3,1,2,0:T(8,128)S(1)}, u32[]{:S(2)}, u32[]{:S(2)}) async-start(f32[8,80,2,192]{3,1,2,0:T(8,128)} %copy.134), calls=%async_computation.5 | async-start | bytes 2621440 | tf_op jit(solution)/shard_map/all_to_all | solution.py:69
  400.6 41.9 %copy-start.4 = (f32[2,320,2,192]{1,3,2,0:T(8,128)S(1)}, f32[2,320,2,192]{1,3,2,0:T(8,128)}, u32[]{:S(2)}) copy-start(f32[2,320,2,192]{1,3,2,0:T(8,128)} %param.10) | copy-start | bytes 2949124
  402.7 43.4 %copy-start.6 = (f32[2,320,1,192]{1,3,0,2:T(8,128)S(1)}, f32[2,320,1,192]{1,3,0,2:T(8,128)}, u32[]{:S(2)}) copy-start(f32[2,320,1,192]{1,3,0,2:T(8,128)} %copy.160) | copy-start | bytes 1474564
  441.8 27.1 %copy-start.1 = (s32[320,192]{0,1:T(8,128)S(1)}, s32[320,192]{0,1:T(8,128)}, u32[]{:S(2)}) copy-start(s32[320,192]{0,1:T(8,128)} %param.7) | copy-start | bytes 737284
  442.5 3.6 copy-start.7
  445.1 22.7 %copy-start.5 = (f32[2,320,2,192]{1,3,0,2:T(8,128)S(1)}, f32[2,320,2,192]{1,3,0,2:T(8,128)}, u32[]{:S(2)}) copy-start(f32[2,320,2,192]{1,3,0,2:T(8,128)} %get-tuple-element.33) | copy-start | bytes 2949124
Sparse Core Ops, SparseCore 0:
  10.7 88.5 all-gather.3
  117.0 84.5 all-gather.7
  298.4 84.9 all-gather.5
where the time goes:
time: 480 us; the launch traced here: 476 us
  blocking collectives  151 us (31%)
  waiting for transfers between devices  134 us (28%)
  matrix products  116 us (24%)
  local copies, waits for them, and re-layouts  36.4 us (8%)
  between operations  17.1 us (4%)
  starting transfers between devices  10.7 us (2%)
  other arithmetic  10.5 us (2%)
    all_gather x1, waiting for transfers between devices, per_device(): lax.all_gather(direction_low, 'rcv', axis=1, tiled=True)  89 us
    dot_general x12, matrix products, contract_time(): return jnp.einsum('tf,frk->trk', table, values, precision=highest)  57 us
    all_to_all x2, blocking collectives, gate(): lax.all_to_all(field, 'freq', split_axis=1, concat_axis=0, tiled=True)  40.3 us
    psum x1, blocking collectives, per_device(): new_gamma = lax.psum(jnp.sum(new_gradient * new_gradient), ('freq', 'rcv'))  39.1 us
    psum x1, blocking collectives, per_device(): gamma = lax.psum(jnp.sum(gradient * gradient), ('freq', 'rcv'))  38.8 us
    dot_general x12, matrix products, contract_back(): return jnp.einsum('tf,trk->frk', table, values, precision=highest)  32.3 us
    all_to_all x2, waiting for transfers between devices, gate(): lax.all_to_all(gated_part, 'freq', split_axis=0, concat_axis=1, tiled=True)  31.3 us
    dot_general x3, matrix products, accumulate(): jnp.einsum('fpnm,fmqk->fpnqk', reflection, piece, preferred_element_type=...  26.4 us
  transfers between devices with their start and end apart: 6, of which 4 were waited for; matrix products, arithmetic and copies ran while one was open for 26% of the time, Pallas kernels for 0%

commit v1 on v0

--- a/solution.py
+++ b/solution.py
@@ -1,3 +1,4 @@
+import functools
 import math
 import jax
 import jax.numpy as jnp
@@ -10,6 +11,43 @@
 band_start = 5
 tiny = 1e-06
 highest = lax.Precision.HIGHEST
+
+
+def part_the_things(x_part, k_dim, mine_x):
+    b_next = x_part.shape
+    g_now = x_part.reshape(*b_next[:k_dim], mine_x, b_next[k_dim] // mine_x, *b_next[k_dim + 1 :])
+    front = jnp.moveaxis(g_now, k_dim, 0)
+    return front
+
+
+def supply_all_turns(mine, array_axis):
+    mine = jnp.moveaxis(mine, 0, array_axis)
+    everything = mine.shape
+    b_now = mine.reshape(
+        *everything[:array_axis],
+        everything[array_axis] * everything[array_axis + 1],
+        *everything[array_axis + 2 :]
+    )
+    return b_now
+
+
+def save_point_for(array_here, axis_tag, content, packet):
+    arr_out = lax.axis_size(axis_tag)
+    arr_now = lax.axis_index(axis_tag)
+    part_next, all_values = (arr_out, arr_now)
+    k_now = part_the_things(array_here, content, part_next)
+    runs = [k_now[all_values]]
+    for ix in range(1, part_next):
+        back = k_now[(all_values + ix) % part_next]
+        runs.append(
+            lax.ppermute(back, axis_tag, [(c, (c + ix) % part_next) for c in range(part_next)])
+        )
+    k_now = jnp.stack(runs, axis=0)[(all_values - jnp.arange(part_next)) % part_next]
+    step_out = supply_all_turns(k_now, packet)
+    return step_out
+
+
+fill_files = functools.partial(save_point_for, axis_tag="freq", content=1, packet=0)
 
 
 def tables(count):
@@ -60,7 +98,7 @@
     cos_table, sin_table = tables(F)
 
     def gate(field, complement):
-        spread = lax.all_to_all(field, "freq", split_axis=1, concat_axis=0, tiled=True)
+        spread = fill_files(field)
         share = local_rows // groups
         limits = lax.dynamic_slice_in_dim(starts, position * share, share, 0)
         gated_part = time_gate(

time: 480 us -> 465 us (0.969)
  blocking collectives: 151 us -> 109 us
  waiting for transfers between devices: 134 us -> 146 us
  starting transfers between devices: 10.7 us -> 17 us
  local copies, waits for them, and re-layouts: 36.4 us -> 41.9 us
    all_to_all x2 -> x0, blocking collectives: 40.3 us -> none  [gate(): lax.all_to_all(field, 'freq', split_axis=1, concat_axis=0, tiled=True)]
    ppermute x0 -> x9, waiting for transfers between devices: none -> 35.3 us  [save_point_for(): lax.ppermute(back, axis_tag, [(c, (c + ix) % part_next) for c in range(pa...]
    all_to_all x1 -> x0, waiting for transfers between devices: 13.3 us -> none  [gate(): lax.all_to_all(field, 'freq', split_axis=1, concat_axis=0, tiled=True)]
    all_to_all x9 -> x0, local copies, waits for them, and re-layouts: 12 us -> none  [gate(): lax.all_to_all(field, 'freq', split_axis=1, concat_axis=0, tiled=True)]
    ppermute x0 -> x9, starting transfers between devices: none -> 9.01 us  [save_point_for(): lax.ppermute(back, axis_tag, [(c, (c + ix) % part_next) for c in range(pa...]
    all_to_all x2, waiting for transfers between devices: 31.3 us -> 23.5 us  [gate(): lax.all_to_all(gated_part, 'freq', split_axis=0, concat_axis=1, tiled=True)]
    gather x0 -> x3, local copies, waits for them, and re-layouts: none -> 6.44 us  [save_point_for(): jnp.stack(runs, axis=0)[(all_values - jnp.arange(part_next)) % part_next]]
    unnamed x26 -> x22, local copies, waits for them, and re-layouts: 9.67 us -> 15.1 us
  transfers between devices with their start and end apart: 6 -> 14, of which waited for: 4 -> 11; matrix products, arithmetic and copies ran while one was open for 26% -> 33% of each run, Pallas kernels for 0% -> 0%
where the time goes in v1:
time: 465 us; the launch traced here: 460 us
  waiting for transfers between devices  146 us (31%)
  matrix products  116 us (25%)
  blocking collectives  109 us (23%)
  local copies, waits for them, and re-layouts  41.9 us (9%)
  between operations  17.2 us (4%)
  starting transfers between devices  17 us (4%)
  other arithmetic  13.6 us (3%)
    all_gather x1, waiting for transfers between devices, per_device(): lax.all_gather(direction_low, 'rcv', axis=1, tiled=True)  86.8 us
    dot_general x12, matrix products, contract_time(): return jnp.einsum('tf,frk->trk', table, values, precision=highest)  57.2 us
    psum x1, blocking collectives, per_device(): gamma = lax.psum(jnp.sum(gradient * gradient), ('freq', 'rcv'))  39.2 us
    psum x1, blocking collectives, per_device(): new_gamma = lax.psum(jnp.sum(new_gradient * new_gradient), ('freq', 'rcv'))  37 us
    ppermute x9, waiting for transfers between devices, save_point_for(): lax.ppermute(back, axis_tag, [(c, (c + ix) % part_next) for c in range(pa...  35.3 us
    dot_general x12, matrix products, contract_back(): return jnp.einsum('tf,trk->frk', table, values, precision=highest)  32.3 us
    dot_general x3, matrix products, accumulate(): jnp.einsum('fpnm,fmqk->fpnqk', reflection, piece, preferred_element_type=...  26.4 us
    all_to_all x2, waiting for transfers between devices, gate(): lax.all_to_all(gated_part, 'freq', split_axis=0, concat_axis=1, tiled=True)  23.5 us
  transfers between devices with their start and end apart: 14, of which 11 were waited for; matrix products, arithmetic and copies ran while one was open for 33% of the time, Pallas kernels for 0%

profile of v1, /device:TPU:0, one launch (start us, length us, event | category | flops | bytes accessed | tf_op | source)
XLA Modules:
  0.0 459.9 jit_solution(3876360536449544174)
XLA Ops:
  12.6 86.8 %all-gather.4.cloned.1.call-done = bf16[2,2560,2,192]{3,2,0,1:T(2,128)(2,1)} async-done(((bf16[2,320,2,192]{3,2,0,1:T(2,128)(2,1)}), bf16[2,2560,2,192]{3,2,0,1:T(2,128)(2,1)}) %all-gather.4.cloned.1.call-update) | async-done | bytes 3932176 | tf_op jit(solution)/shard_map/all_gather | solution.py:114
  99.4 8.1 %fusion.4 = f32[2,2,320,2,192]{2,4,3,1,0:T(8,128)S(1)} fusion(bf16[2,2,320,2560]{3,2,1,0:T(8,128)(2,1)} %param.6, bf16[2,2560,2,192,1]{3,2,0,1,4:T(2,128)(2,1)} %bitcast.228), kind=kOutput, calls=%fused_computation.7 | convolution fusion | flops 2516582400 | bytes 12451840 | tf_op jit(solution)/shard_map/fpnm,fmqk->fpnqk/dot_general | solution.py:110
  113.1 5.5 %collective-permute-done.1 = f32[2,80,2,192]{3,1,2,0:T(8,128)S(1)} collective-permute-done((f32[2,80,2,192]{3,1,2,0:T(8,128)}, f32[2,80,2,192]{3,1,2,0:T(8,128)S(1)}, u32[]{:S(2)}, u32[]{:S(2)}) %collective-permute-start.1) | collective-permute-done | bytes 245792 | tf_op jit(solution)/shard_map/ppermute | solution.py:43
  118.6 4.6 %collective-permute-done.2 = f32[2,80,2,192]{3,1,2,0:T(8,128)S(1)} collective-permute-done((f32[2,80,2,192]{3,1,2,0:T(8,128)}, f32[2,80,2,192]{3,1,2,0:T(8,128)S(1)}, u32[]{:S(2)}, u32[]{:S(2)}) %collective-permute-start.2) | collective-permute-done | bytes 245792 | tf_op jit(solution)/shard_map/ppermute | solution.py:43
  128.3 4.4 fusion.30
  132.7 4.4 fusion.29
  137.1 5.0 %subtract_select_fusion.1 = f32[64,80,192]{2,0,1:T(8,128)S(1)} fusion(f32[64,80,192]{2,0,1:T(8,128)S(1)} %fusion.30, s32[80,192]{1,0:T(8,128)S(1)} %copy.89, f32[8,80,1,192]{3,1,2,0:T(8,128)S(1)} %get-tuple-element.45, f32[8]{0:T(128)S(1)} %add_convert_fusion, f32[64]{0:T(128)S(1)} %iota_multiply_fusion), kind=kOutput, calls=%fused_computation.18 | convolution fusion | flops 97321984 | bytes 8417568 | tf_op jit(solution)/shard_map/tf,frk->trk/dot_general | solution.py:61
  144.8 4.9 %add_select_fusion.1 = f32[64,80,192]{2,0,1:T(8,128)S(1)} fusion(f32[64,80,192]{2,0,1:T(8,128)S(1)} %fusion.29, s32[80,192]{1,0:T(8,128)S(1)} %copy.89, f32[8,80,1,192]{3,1,2,0:T(8,128)S(1)} %get-tuple-element.45, f32[8]{0:T(128)S(1)} %add_convert_fusion, f32[64]{0:T(128)S(1)} %iota_multiply_fusion), kind=kOutput, calls=%fused_computation.17 | convolution fusion | flops 97321984 | bytes 8417568 | tf_op jit(solution)/shard_map/tf,frk->trk/dot_general | solution.py:61
  159.5 3.5 all-to-all-start
  165.2 15.4 %all-to-all-done = f32[8,80,2,192]{3,1,2,0:T(8,128)S(1)} async-done(((f32[8,80,2,192]{3,1,2,0:T(8,128)}), f32[8,80,2,192]{3,1,2,0:T(8,128)S(1)}, u32[]{:S(2)}, u32[]{:S(2)}) %all-to-all-start) | async-done | bytes 983072 | tf_op jit(solution)/shard_map/all_to_all | solution.py:107
  184.4 39.2 %all-reduce = (f32[]{:T(128)}, f32[]{:T(128)}) all-reduce(f32[]{:T(128)} %multiply_reduce_fusion.2, f32[]{:T(128)} %multiply_reduce_fusion), channel_id=1, replica_groups=mesh['freq'=4,'rcv'=8] {'freq','rcv'}, use_global_device_ids=true, to_apply=%region_1.0 | all-reduce | flops 2 | bytes 16 | tf_op jit(solution)/shard_map/psum | solution.py:116
  230.7 5.0 %collective-permute-done.3 = f32[2,80,2,192]{3,1,2,0:T(8,128)S(1)} collective-permute-done((f32[2,80,2,192]{3,1,2,0:T(8,128)S(1)}, f32[2,80,2,192]{3,1,2,0:T(8,128)S(1)}, u32[]{:S(2)}, u32[]{:S(2)}) %collective-permute-start.3) | collective-permute-done | bytes 245792 | tf_op jit(solution)/shard_map/ppermute | solution.py:43
  237.5 5.9 %collective-permute-done.5 = f32[2,80,2,192]{3,1,2,0:T(8,128)S(1)} collective-permute-done((f32[2,80,2,192]{3,1,2,0:T(8,128)S(1)}, f32[2,80,2,192]{3,1,2,0:T(8,128)S(1)}, u32[]{:S(2)}, u32[]{:S(2)}) %collective-permute-start.5) | collective-permute-done | bytes 245792 | tf_op jit(solution)/shard_map/ppermute | solution.py:43
  244.7 3.0 gather_fusion.1
  249.0 4.4 fusion.32
  253.5 4.4 fusion.31
  257.9 5.1 %subtract_select_fusion = f32[64,80,192]{2,0,1:T(8,128)S(1)} fusion(f32[64,80,192]{2,0,1:T(8,128)S(1)} %fusion.32, s32[80,192]{1,0:T(8,128)S(1)} %copy.89, f32[8,80,1,192]{3,1,2,0:T(8,128)S(1)} %get-tuple-element.39, f32[8]{0:T(128)S(1)} %add_convert_fusion, f32[64]{0:T(128)S(1)} %iota_multiply_fusion), kind=kOutput, calls=%fused_computation.16 | convolution fusion | flops 97321984 | bytes 8417568 | tf_op jit(solution)/shard_map/tf,frk->trk/dot_general | solution.py:61
  265.6 4.9 %add_select_fusion = f32[64,80,192]{2,0,1:T(8,128)S(1)} fusion(f32[64,80,192]{2,0,1:T(8,128)S(1)} %fusion.31, s32[80,192]{1,0:T(8,128)S(1)} %copy.89, f32[8,80,1,192]{3,1,2,0:T(8,128)S(1)} %get-tuple-element.39, f32[8]{0:T(128)S(1)} %add_convert_fusion, f32[64]{0:T(128)S(1)} %iota_multiply_fusion), kind=kOutput, calls=%fused_computation.15 | convolution fusion | flops 97321984 | bytes 8417568 | tf_op jit(solution)/shard_map/tf,frk->trk/dot_general | solution.py:61
  278.8 13.2 %all_to_all.36 = bf16[8,80,2,192]{3,1,2,0:T(8,128)(2,1)S(1)} all-to-all(bf16[8,80,2,192]{3,1,2,0:T(8,128)(2,1)S(1)} %copy.105), channel_id=1, replica_groups=mesh['freq'=4,'rcv'=8] {'freq'}, dimensions={0} | all-to-all | bytes 983040 | tf_op jit(solution)/shard_map/all_to_all | solution.py:107
  293.6 8.1 %fusion.2 = f32[2,2,320,2,192]{2,4,3,1,0:T(8,128)S(1)} fusion(bf16[2,2,320,2560]{3,2,1,0:T(8,128)(2,1)} %param.6, bf16[2,2560,2,192,1]{3,2,0,1,4:T(2,128)(2,1)} %bitcast.226), kind=kOutput, calls=%fused_computation.5 | convolution fusion | flops 2516582400 | bytes 12451840 | tf_op jit(solution)/shard_map/fpnm,fmqk->fpnqk/dot_general | solution.py:110
  310.1 6.9 %collective-permute-done.6 = f32[2,80,2,192]{3,1,2,0:T(8,128)S(1)} collective-permute-done((f32[2,80,2,192]{3,1,2,0:T(8,128)S(1)}, f32[2,80,2,192]{3,1,2,0:T(8,128)S(1)}, u32[]{:S(2)}, u32[]{:S(2)}) %collective-permute-start.6) | collective-permute-done | bytes 245792 | tf_op jit(solution)/shard_map/ppermute | solution.py:43
  318.3 4.3 collective-permute-done.8
  325.8 4.4 fusion.34
  330.2 4.4 fusion.33
  334.6 5.5 %subtract_multiply_fusion = f32[64,80,192]{2,0,1:T(8,128)S(1)} fusion(f32[64,80,192]{2,0,1:T(8,128)S(1)} %fusion.34, s32[80,192]{1,0:T(8,128)S(1)} %copy.89, f32[8,80,1,192]{3,1,2,0:T(8,128)S(1)} %get-tuple-element.33, f32[8]{0:T(128)S(1)} %add_convert_fusion, f32[64]{0:T(128)S(1)} %iota_multiply_fusion), kind=kOutput, calls=%fused_computation.13 | convolution fusion | flops 99288064 | bytes 8417568 | tf_op jit(solution)/shard_map/tf,frk->trk/dot_general | solution.py:61
  342.8 5.3 %add_multiply_fusion = f32[64,80,192]{2,0,1:T(8,128)S(1)} fusion(f32[64,80,192]{2,0,1:T(8,128)S(1)} %fusion.33, s32[80,192]{1,0:T(8,128)S(1)} %copy.89, f32[8,80,1,192]{3,1,2,0:T(8,128)S(1)} %get-tuple-element.33, f32[8]{0:T(128)S(1)} %add_convert_fusion, f32[64]{0:T(128)S(1)} %iota_multiply_fusion), kind=kOutput, calls=%fused_computation.12 | convolution fusion | flops 99288064 | bytes 8417568 | tf_op jit(solution)/shard_map/tf,frk->trk/dot_general | solution.py:61
  350.8 2.8 fusion.54
  357.8 4.3 all-to-all-start.2
  371.9 8.1 %all-to-all-done.2 = f32[8,80,2,192]{3,1,2,0:T(8,128)} async-done(((f32[8,80,2,192]{3,1,2,0:T(8,128)}), f32[8,80,2,192]{3,1,2,0:T(8,128)}, u32[]{:S(2)}, u32[]{:S(2)}) %all-to-all-start.2) | async-done | bytes 983072 | tf_op jit(solution)/shard_map/all_to_all | solution.py:107
  383.1 19.3 %psum.31 = f32[2,2,192]{2,0,1:T(2,128)S(1)} all-reduce(f32[2,2,192]{2,0,1:T(2,128)S(1)} %pad_maximum_fusion.8), channel_id=1, replica_groups=mesh['freq'=4,'rcv'=8] {'rcv'}, use_global_device_ids=true, to_apply=%region_8.9 | all-reduce | flops 768 | bytes 6144 | tf_op jit(solution)/shard_map/psum | solution.py:139
  402.4 10.2 %fusion.9 = f32[2,2,320,2,192]{2,4,1,3,0:T(8,128)S(1)} fusion(bf16[2,2,320,2560]{3,2,1,0:T(8,128)(2,1)} %param.6, bf16[2,2560,2,192,1]{3,2,0,1,4:T(2,128)(2,1)} %bitcast.227), kind=kOutput, calls=%fused_computation.29 | convolution fusion | flops 2516582400 | bytes 12451840 | tf_op jit(solution)/shard_map/fpnm,fmqk->fpnqk/dot_general | solution.py:110
  414.2 37.0 %psum.30 = f32[]{:T(128)} all-reduce(f32[]{:T(128)} %multiply_reduce_fusion.1), channel_id=1, replica_groups=mesh['freq'=4,'rcv'=8] {'freq','rcv'}, use_global_device_ids=true, to_apply=%region_5.6 | all-reduce | flops 1 | bytes 8 | tf_op jit(solution)/shard_map/psum | solution.py:125
  (111 shorter events, 94.4 us)
Async XLA Ops:
  7.2 5.4 %copy-start = (s32[320,192]{0,1:T(8,128)S(1)}, s32[320,192]{0,1:T(8,128)}, u32[]{:S(2)}) copy-start(s32[320,192]{0,1:T(8,128)} %param.7) | copy-start | bytes 737284
  7.2 3.4 copy-start.5
  7.2 92.2 %all-gather.4.cloned.1.call-start = ((), (), s32[]{:S(2)}) async-start(), calls=%async_computation.3 | async-start | bytes 5898240 | tf_op jit(solution)/shard_map/all_gather | solution.py:114
  10.5 283.1 %all-gather.8.cloned.1.call-start = ((), (), s32[]{:S(2)}) async-start(), calls=%async_computation.5 | async-start | bytes 5898240 | tf_op jit(solution)/shard_map/all_gather | solution.py:127
  109.0 9.6 %collective-permute-start.1 = (f32[2,80,2,192]{3,1,2,0:T(8,128)}, f32[2,80,2,192]{3,1,2,0:T(8,128)S(1)}, u32[]{:S(2)}, u32[]{:S(2)}) collective-permute-start(f32[2,80,2,192]{3,1,2,0:T(8,128)} %bitcast.193), channel_id=1, source_target_pairs={{0,16},{8,24},{16,0},{24,8},{1,17},{9,25},{17,1},{25,9},{2,18},{10... | collective-permute-start | bytes 737288 | tf_op jit(solution)/shard_map/ppermute | solution.py:43
  111.3 12.0 %collective-permute-start.2 = (f32[2,80,2,192]{3,1,2,0:T(8,128)}, f32[2,80,2,192]{3,1,2,0:T(8,128)S(1)}, u32[]{:S(2)}, u32[]{:S(2)}) collective-permute-start(f32[2,80,2,192]{3,1,2,0:T(8,128)} %bitcast.192), channel_id=1, source_target_pairs={{0,24},{8,0},{16,8},{24,16},{1,25},{9,1},{17,9},{25,17},{2,26},{10... | collective-permute-start | bytes 737288 | tf_op jit(solution)/shard_map/ppermute | solution.py:43
  112.0 11.3 %collective-permute-start = (f32[2,80,2,192]{3,1,2,0:T(8,128)}, f32[2,80,2,192]{3,1,2,0:T(8,128)}, u32[]{:S(2)}, u32[]{:S(2)}) collective-permute-start(f32[2,80,2,192]{3,1,2,0:T(8,128)} %bitcast.194), channel_id=1, source_target_pairs={{0,8},{8,16},{16,24},{24,0},{1,9},{9,17},{17,25},{25,1},{2,10},{10... | collective-permute-start | bytes 737288 | tf_op jit(solution)/shard_map/ppermute | solution.py:43
  123.3 0.7 copy-start.6
  159.5 21.2 %all-to-all-start = ((f32[8,80,2,192]{3,1,2,0:T(8,128)}), f32[8,80,2,192]{3,1,2,0:T(8,128)S(1)}, u32[]{:S(2)}, u32[]{:S(2)}) async-start(f32[8,80,2,192]{3,1,2,0:T(8,128)} %copy.99), calls=%async_computation | async-start | bytes 2621440 | tf_op jit(solution)/shard_map/all_to_all | solution.py:107
  163.0 239.4 %all-gather.6.cloned.1.call-start = ((), (), s32[]{:S(2)}) async-start(), calls=%async_computation.4 | async-start | bytes 5898240 | tf_op jit(solution)/shard_map/all_gather | solution.py:123
  224.9 1.3 copy-start.4
  226.5 9.2 %collective-permute-start.3 = (f32[2,80,2,192]{3,1,2,0:T(8,128)S(1)}, f32[2,80,2,192]{3,1,2,0:T(8,128)S(1)}, u32[]{:S(2)}, u32[]{:S(2)}) collective-permute-start(f32[2,80,2,192]{3,1,2,0:T(8,128)S(1)} %get-tuple-element.44), channel_id=1, source_target_pairs={{0,8},{8,16},{16,24},{24,0},{1,9},{9,17},{17,25},{25,1},{2,10},{10... | collective-permute-start | bytes 737288 | tf_op jit(solution)/shard_map/ppermute | solution.py:43
  226.6 10.9 %collective-permute-start.4 = (f32[2,80,2,192]{3,1,2,0:T(8,128)S(1)}, f32[2,80,2,192]{3,1,2,0:T(8,128)S(1)}, u32[]{:S(2)}, u32[]{:S(2)}) collective-permute-start(f32[2,80,2,192]{3,1,2,0:T(8,128)S(1)} %get-tuple-element.43), channel_id=1, source_target_pairs={{0,16},{8,24},{16,0},{24,8},{1,17},{9,25},{17,1},{25,9},{2,18},{10... | collective-permute-start | bytes 737288 | tf_op jit(solution)/shard_map/ppermute | solution.py:43
  228.9 14.5 %collective-permute-start.5 = (f32[2,80,2,192]{3,1,2,0:T(8,128)S(1)}, f32[2,80,2,192]{3,1,2,0:T(8,128)S(1)}, u32[]{:S(2)}, u32[]{:S(2)}) collective-permute-start(f32[2,80,2,192]{3,1,2,0:T(8,128)S(1)} %get-tuple-element.42), channel_id=1, source_target_pairs={{0,24},{8,0},{16,8},{24,16},{1,25},{9,1},{17,9},{25,17},{2,26},{10... | collective-permute-start | bytes 737288 | tf_op jit(solution)/shard_map/ppermute | solution.py:43
  307.6 9.4 %collective-permute-start.6 = (f32[2,80,2,192]{3,1,2,0:T(8,128)S(1)}, f32[2,80,2,192]{3,1,2,0:T(8,128)S(1)}, u32[]{:S(2)}, u32[]{:S(2)}) collective-permute-start(f32[2,80,2,192]{3,1,2,0:T(8,128)S(1)} %bitcast.221), channel_id=1, source_target_pairs={{0,8},{8,16},{16,24},{24,0},{1,9},{9,17},{17,25},{25,1},{2,10},{10... | collective-permute-start | bytes 737288 | tf_op jit(solution)/shard_map/ppermute | solution.py:43
  307.7 10.6 %collective-permute-start.7 = (f32[2,80,2,192]{3,1,2,0:T(8,128)S(1)}, f32[2,80,2,192]{3,1,2,0:T(8,128)S(1)}, u32[]{:S(2)}, u32[]{:S(2)}) collective-permute-start(f32[2,80,2,192]{3,1,2,0:T(8,128)S(1)} %bitcast.222), channel_id=1, source_target_pairs={{0,16},{8,24},{16,0},{24,8},{1,17},{9,25},{17,1},{25,9},{2,18},{10... | collective-permute-start | bytes 737288 | tf_op jit(solution)/shard_map/ppermute | solution.py:43
  308.2 14.4 %collective-permute-start.8 = (f32[2,80,2,192]{3,1,2,0:T(8,128)S(1)}, f32[2,80,2,192]{3,1,2,0:T(8,128)S(1)}, u32[]{:S(2)}, u32[]{:S(2)}) collective-permute-start(f32[2,80,2,192]{3,1,2,0:T(8,128)S(1)} %bitcast.223), channel_id=1, source_target_pairs={{0,24},{8,0},{16,8},{24,16},{1,25},{9,1},{17,9},{25,17},{2,26},{10... | collective-permute-start | bytes 737288 | tf_op jit(solution)/shard_map/ppermute | solution.py:43
  356.3 5.8 %copy-start.2 = (f32[2,320,2,192]{1,3,2,0:T(8,128)S(1)}, f32[2,320,2,192]{1,3,2,0:T(8,128)}, u32[]{:S(2)}) copy-start(f32[2,320,2,192]{1,3,2,0:T(8,128)} %param.10) | copy-start | bytes 2949124
  357.8 22.1 %all-to-all-start.2 = ((f32[8,80,2,192]{3,1,2,0:T(8,128)}), f32[8,80,2,192]{3,1,2,0:T(8,128)}, u32[]{:S(2)}, u32[]{:S(2)}) async-start(f32[8,80,2,192]{3,1,2,0:T(8,128)} %copy.121), calls=%async_computation.2 | async-start | bytes 2621440 | tf_op jit(solution)/shard_map/all_to_all | solution.py:107
  412.6 39.4 %copy-start.3 = (f32[2,320,2,192]{1,3,2,0:T(8,128)S(1)}, f32[2,320,2,192]{1,3,2,0:T(8,128)}, u32[]{:S(2)}) copy-start(f32[2,320,2,192]{1,3,2,0:T(8,128)} %param.10) | copy-start | bytes 2949124
  451.2 1.9 copy-start.1
Sparse Core Ops, SparseCore 0:
  10.8 88.5 all-gather.3
  102.2 84.1 all-gather.7
  293.7 84.1 all-gather.5
